TPU v7x, 32 devices: a whole 2x2x4 slice. The times are simulated.
32 devices in a mesh: grp: 2 (over y), gx: 4 (over z), gy: 2 (over x), row: 2 (over core).
Axes of the slice: x: 2, y: 2, z: 4, core: 2. Of those that a mesh axis runs over, the one named last changes fastest.
Arguments:
- conc: float32 [64, 8, 16, 128], P(None, ('grp', 'gx'), ('gy', 'row')), parts along dimension 1, may hold values from 0.2 to 2
- cotangent: float32 [64, 8, 16, 128], P(None, ('grp', 'gx'), ('gy', 'row')), parts along dimension 1, may hold values from -6 to 6
- courant: float32 [32, 128], P(('grp', 'gy', 'row')), parts along dimension 0, may hold values from 8 to 100
- direction: int32 [32, 128], P(('grp', 'gy', 'row')), parts along dimension 0, may hold values 0 or 1
- rate_const: float32 [1024], replicated, may hold values from 0.01 to 0.1
- orders: int32 [1024, 64], replicated, may hold values from 0 to 2, as said below
- stoich: int32 [64, 1024], replicated, may hold values from -2 to 1, as said below
Outputs:
- final_state: float32 [64, 8, 16, 128], P(None, ('grp', 'gx'), ('gy', 'row')), parts along dimension 1
- adjoint: float32 [64, 8, 16, 128], P(None, ('grp', 'gx'), ('gy', 'row')), parts along dimension 1
There are 2 independent parts, one for each index of `grp`. A program takes and returns all parts, laid end to end along the dimension named above; an argument that names none is the same for every part. Nothing has to cross between parts.
Inputs may be any that keep to these rules, and one draw needn't show every extreme that they name: `orders`: each reaction has two different reactants, each of order 1 or 2, and no other nonzero order. stoich[s, j] is 1 for the product species of reaction j (one species) minus orders[j, s].
All inputs are finite; a program needn't handle non-finite values. No bound on the sum of `direction` on one device may be relied on, other than what follows from the above.
Results may differ from a plain program's by a relative error of at most 0.0003.
Values sent between devices are 32-bit elements; how exact they have to be, the bound alone decides.
No kernel may reach another device: no remote copies, remote signals or barrier semaphores. Data moves between devices by JAX's collectives and lax.ppermute only.
A program may use at most 64 MiB of HBM per device.

v0:
```python
import jax
import jax.numpy as jnp
from jax import lax
from jax.sharding import PartitionSpec as P

STEPS = 2


time_step = 0.1
diffusion = 0.1
highest = lax.Precision.HIGHEST


def padded_2(block, sides, width):
    for axis, dim in sides:
        count = lax.axis_size(axis)
        forward = [(i, i + 1) for i in range(count - 1)]
        backward = [(target, source) for source, target in forward]
        low = lax.ppermute(
            lax.slice_in_dim(block, block.shape[dim] - width, None, axis=dim), axis, forward
        )
        high = lax.ppermute(lax.slice_in_dim(block, 0, width, axis=dim), axis, backward)
        block = jnp.concatenate([low, block, high], axis=dim)
    return block


def combine_pairs(leading, trailing):
    return (leading[0] * trailing[0], trailing[0] * leading[1] + trailing[1])


def recurrence(values, weight, backward):
    multipliers = jnp.broadcast_to(weight[None, None], (1, values.shape[1]) + weight.shape)
    return lax.associative_scan(combine_pairs, (multipliers, values), reverse=backward, axis=1)


def sweep_fields(fields, weight, mask):
    stacked = jnp.stack(fields)
    pencils = lax.all_to_all(stacked, "gx", split_axis=1, concat_axis=2, tiled=True)
    rising = recurrence(pencils[0], weight, False)[1]
    falling = recurrence(pencils[-1], weight, True)[1]
    results = jnp.stack([jnp.where(mask, rising, falling)])
    back = lax.all_to_all(results, "gx", split_axis=2, concat_axis=1, tiled=True)
    return [back[0]]


def sweep(values, weight, upward):
    return sweep_fields([values], weight, upward[None, None])[0]


def smooth_padded(values, padded):
    widths = [(0, 0)] * (padded.ndim - 1) + [(1, 1)]
    padded = jnp.pad(padded, widths)
    beside_all = (
        padded[..., 2:, 1:-1]
        + padded[..., :-2, 1:-1]
        + padded[..., 1:-1, 2:]
        + padded[..., 1:-1, :-2]
    )
    return values + diffusion * (beside_all - 4.0 * values)


def smooth(values):
    padded = padded_2(values, ((("gy", "row"), 2),), 1)
    return smooth_padded(values, padded)


def reaction_rates(cells, order_float, rate_const):
    activity = 0.5 * jnp.log1p(cells * cells)
    return rate_const[:, None] * jnp.exp(jnp.dot(order_float, activity, precision=highest))


def per_slice(function, arrays, shape):
    species, depth = (shape[0], shape[1])
    flats = [item.reshape(species, -1) for item in arrays]
    pieces = function(*[item for item in flats])
    return pieces.reshape(shape)


def shards(conc, cotangent, courant, direction, rate_const, orders, stoich):
    order_float = orders.astype(jnp.float32)
    stoich_float = stoich.astype(jnp.float32)
    order_trans = order_float.T
    stoich_trans = stoich_float.T
    retain = courant / (1.0 + courant)
    admit = 1.0 / (1.0 + courant)

    def react(cells):
        return cells + time_step * jnp.dot(
            stoich_float, reaction_rates(cells, order_float, rate_const), precision=highest
        )

    def react_back(cells, spread):
        rates = reaction_rates(cells, order_float, rate_const)
        pulled = jnp.dot(stoich_trans, spread, precision=highest)
        summed = jnp.dot(order_trans, rates * pulled, precision=highest)
        return spread + time_step * cells / (1.0 + cells * cells) * summed

    upward = direction == 1
    states = [conc]
    for position in range(STEPS):
        current = states[-1]
        starred = per_slice(react, [current], current.shape)
        states.append(sweep(admit * smooth(starred), retain, upward))
    adjoint = cotangent
    for position in reversed(range(STEPS)):
        carried = admit * sweep(adjoint, retain, direction == 0)
        spread = smooth(carried)
        adjoint = per_slice(react_back, [states[position], spread], spread.shape)
    return (states[-1], adjoint)


def solution(mesh):
    placed = (
        P(None, ("grp", "gx"), ("gy", "row"), None),
        P(None, ("grp", "gx"), ("gy", "row"), None),
        P(("grp", "gy", "row"), None),
        P(("grp", "gy", "row"), None),
        P(),
        P(),
        P(),
    )
    return jax.shard_map(
        shards,
        mesh=mesh,
        in_specs=placed,
        out_specs=(
            P(None, ("grp", "gx"), ("gy", "row"), None),
            P(None, ("grp", "gx"), ("gy", "row"), None),
        ),
        check_vma=False,
    )
```

profile of v0, /device:TPU:2, one launch (start us, length us, event | category | flops | bytes accessed | tf_op | source)
XLA Modules:
  0.0 119.4 jit_solution(14529348477892977606)
XLA Ops:
  0.7 2.9 %fusion.45 = f32[512,1024]{1,0:T(8,128)S(1)} fusion(s32[1024,64]{0,1:T(8,128)} %param.12, f32[8,8,4,128]{3,2,1,0:T(4,128)} %bitcast.141), kind=kOutput, calls=%fused_computation.45 | convolution fusion | flops 402784256 | bytes 2490368 | tf_op jit(solution)/shard_map/dot_general | solution.py:69
  3.6 2.4 %fusion.11 = f32[64,512]{1,0:T(8,128)S(1)} fusion(f32[512,1024]{1,0:T(8,128)S(1)} %fusion.45, f32[1024]{0:T(1024)S(1)} %copy-done.5, s32[64,1024]{1,0:T(8,128)S(1)} %copy-done.2, f32[8,8,4,128]{3,2,1,0:T(4,128)S(1)} %bitcast.142), kind=kOutput, calls=%fused_computation.13 | convolution fusion | flops 403308544 | bytes 2625536 | tf_op jit(solution)/shard_map/dot_general | solution.py:88
  6.1 1.9 %collective-permute-start = (f32[64,1,1,128]{3,2,0,1:T(1,128)S(1)}, f32[64,1,1,128]{3,2,0,1:T(1,128)S(1)}, u32[]{:S(2)}, u32[]{:S(2)}) collective-permute-start(f32[64,1,1,128]{3,2,0,1:T(1,128)S(1)} %get-tuple-element.49), channel_id=1, source_target_pairs={{1,0},{2,1},{3,2},{5,4},{6,5},{7,6},{9,8},{10,9},{11,10},{13,12},{... | collective-permute-start | bytes 98312 | tf_op jit(solution)/shard_map/ppermute | solution.py:22
  8.0 2.4 %collective-permute-start.1 = (f32[64,1,1,128]{3,2,0,1:T(1,128)S(1)}, f32[64,1,1,128]{3,2,0,1:T(1,128)S(1)}, u32[]{:S(2)}, u32[]{:S(2)}) collective-permute-start(f32[64,1,1,128]{3,2,0,1:T(1,128)S(1)} %get-tuple-element.48), channel_id=1, source_target_pairs={{0,1},{1,2},{2,3},{4,5},{5,6},{6,7},{8,9},{9,10},{10,11},{12,13},{... | collective-permute-start | bytes 98312 | tf_op jit(solution)/shard_map/ppermute | solution.py:19
  10.5 4.9 %all-to-all-start.4 = ((f32[1,64,1,4,128]{4,3,2,0,1:T(4,128)}), f32[1,64,1,4,128]{4,3,2,0,1:T(4,128)S(1)}, u32[]{:S(2)}, u32[]{:S(2)}) async-start(f32[1,64,1,4,128]{4,3,2,0,1:T(4,128)} %bitcast.26), calls=%async_computation.4 | async-start | bytes 262144 | tf_op jit(solution)/shard_map/all_to_all | solution.py:38
  16.8 4.4 %all-to-all-done.4 = f32[1,64,1,4,128]{4,3,2,0,1:T(4,128)S(1)} async-done(((f32[1,64,1,4,128]{4,3,2,0,1:T(4,128)}), f32[1,64,1,4,128]{4,3,2,0,1:T(4,128)S(1)}, u32[]{:S(2)}, u32[]{:S(2)}) %all-to-all-start.4) | async-done | bytes 131104 | tf_op jit(solution)/shard_map/all_to_all | solution.py:38
  21.2 3.3 %all-to-all-start = ((f32[1,64,1,4,128]{4,3,2,0,1:T(4,128)}), f32[1,64,1,4,128]{4,3,2,0,1:T(4,128)S(1)}, u32[]{:S(2)}, u32[]{:S(2)}) async-start(f32[1,64,1,4,128]{4,3,2,0,1:T(4,128)} %fusion.69), calls=%async_computation | async-start | bytes 262144 | tf_op jit(solution)/shard_map/all_to_all | solution.py:38
  25.2 5.3 %all-to-all-done = f32[1,64,1,4,128]{4,3,2,0,1:T(4,128)S(1)} async-done(((f32[1,64,1,4,128]{4,3,2,0,1:T(4,128)}), f32[1,64,1,4,128]{4,3,2,0,1:T(4,128)S(1)}, u32[]{:S(2)}, u32[]{:S(2)}) %all-to-all-start) | async-done | bytes 131104 | tf_op jit(solution)/shard_map/all_to_all | solution.py:38
  34.5 3.3 %all-to-all-start.1 = ((f32[1,16,4,4,128]{4,3,1,0,2:T(4,128)}), f32[1,16,4,4,128]{4,3,1,0,2:T(4,128)S(1)}, u32[]{:S(2)}, u32[]{:S(2)}) async-start(f32[1,16,4,4,128]{4,3,1,0,2:T(4,128)} %select_bitcast_fusion.3), calls=%async_computation.1 | async-start | bytes 262144 | tf_op jit(solution)/shard_map/all_to_all | solution.py:42
  43.7 3.8 %all-to-all-start.5 = ((f32[1,16,4,4,128]{4,3,1,0,2:T(4,128)}), f32[1,16,4,4,128]{4,3,1,0,2:T(4,128)S(1)}, u32[]{:S(2)}, u32[]{:S(2)}) async-start(f32[1,16,4,4,128]{4,3,1,0,2:T(4,128)} %select_bitcast_fusion.1), calls=%async_computation.5 | async-start | bytes 262144 | tf_op jit(solution)/shard_map/all_to_all | solution.py:42
  47.5 1.8 %fusion.43 = f32[512,1024]{1,0:T(8,128)S(1)} fusion(s32[1024,64]{0,1:T(8,128)S(1)} %copy-done.3, f32[8,8,4,128]{3,2,1,0:T(4,128)S(1)} %bitcast.135), kind=kOutput, calls=%fused_computation.43 | convolution fusion | flops 402784256 | bytes 2490368 | tf_op jit(solution)/shard_map/dot_general | solution.py:69
  50.8 2.4 %fusion.8 = f32[64,512]{1,0:T(8,128)S(1)} fusion(f32[512,1024]{1,0:T(8,128)S(1)} %fusion.43, f32[1024]{0:T(1024)S(1)} %copy-done.5, s32[64,1024]{1,0:T(8,128)S(1)} %copy-done.2, f32[8,8,4,128]{3,2,1,0:T(4,128)S(1)} %bitcast.136), kind=kOutput, calls=%fused_computation.10 | convolution fusion | flops 403308544 | bytes 2625536 | tf_op jit(solution)/shard_map/dot_general | solution.py:88
  53.2 1.9 %collective-permute-start.2 = (f32[64,1,1,128]{3,2,0,1:T(1,128)S(1)}, f32[64,1,1,128]{3,2,0,1:T(1,128)S(1)}, u32[]{:S(2)}, u32[]{:S(2)}) collective-permute-start(f32[64,1,1,128]{3,2,0,1:T(1,128)S(1)} %get-tuple-element.40), channel_id=1, source_target_pairs={{1,0},{2,1},{3,2},{5,4},{6,5},{7,6},{9,8},{10,9},{11,10},{13,12},{... | collective-permute-start | bytes 98312 | tf_op jit(solution)/shard_map/ppermute | solution.py:22
  55.1 2.4 %collective-permute-start.3 = (f32[64,1,1,128]{3,2,0,1:T(1,128)S(1)}, f32[64,1,1,128]{3,2,0,1:T(1,128)S(1)}, u32[]{:S(2)}, u32[]{:S(2)}) collective-permute-start(f32[64,1,1,128]{3,2,0,1:T(1,128)S(1)} %get-tuple-element.39), channel_id=1, source_target_pairs={{0,1},{1,2},{2,3},{4,5},{5,6},{6,7},{8,9},{9,10},{10,11},{12,13},{... | collective-permute-start | bytes 98312 | tf_op jit(solution)/shard_map/ppermute | solution.py:19
  57.6 2.8 %collective-permute-done.3 = f32[64,1,1,128]{3,2,0,1:T(1,128)S(1)} collective-permute-done((f32[64,1,1,128]{3,2,0,1:T(1,128)S(1)}, f32[64,1,1,128]{3,2,0,1:T(1,128)S(1)}, u32[]{:S(2)}, u32[]{:S(2)}) %collective-permute-start.3) | collective-permute-done | bytes 32800 | tf_op jit(solution)/shard_map/ppermute | solution.py:19
  61.7 2.0 %broadcast_multiply_fusion.1 = (f32[64,1,4,128]{3,2,0,1:T(4,128)S(1)}, f32[1,64,1,4,128]{4,3,2,0,1:T(4,128)}) fusion(f32[64,1,4,128]{3,2,0,1:T(4,128)S(1)} %bitcast.159, f32[4,128]{1,0:T(4,128)S(1)} %copy-done.9, f32[64,1,4,128]{3,2,0,1:T(4,128)S(1)} %reshape.117, f32[64,1,6,130]{3,2,0,1:T(8,128)} %select_maximum_fusion.4, ...), kind=kLoop, calls=%fused_computation.146 | loop fusion | flops 360448 | bytes 854016 | tf_op jit(solution)/shard_map/mul | solution.py:106
  63.8 1.9 %collective-permute-start.4 = (f32[64,1,1,128]{3,2,0,1:T(1,128)S(1)}, f32[64,1,1,128]{3,2,0,1:T(1,128)S(1)}, u32[]{:S(2)}, u32[]{:S(2)}) collective-permute-start(f32[64,1,1,128]{3,2,0,1:T(1,128)S(1)} %get-tuple-element.24), channel_id=1, source_target_pairs={{1,0},{2,1},{3,2},{5,4},{6,5},{7,6},{9,8},{10,9},{11,10},{13,12},{... | collective-permute-start | bytes 98312 | tf_op jit(solution)/shard_map/ppermute | solution.py:22
  65.7 2.4 %collective-permute-start.5 = (f32[64,1,1,128]{3,2,0,1:T(1,128)S(1)}, f32[64,1,1,128]{3,2,0,1:T(1,128)S(1)}, u32[]{:S(2)}, u32[]{:S(2)}) collective-permute-start(f32[64,1,1,128]{3,2,0,1:T(1,128)S(1)} %get-tuple-element.23), channel_id=1, source_target_pairs={{0,1},{1,2},{2,3},{4,5},{5,6},{6,7},{8,9},{9,10},{10,11},{12,13},{... | collective-permute-start | bytes 98312 | tf_op jit(solution)/shard_map/ppermute | solution.py:19
  68.1 5.1 %all-to-all-start.2 = ((f32[1,64,1,4,128]{4,3,2,0,1:T(4,128)}), f32[1,64,1,4,128]{4,3,2,0,1:T(4,128)S(1)}, u32[]{:S(2)}, u32[]{:S(2)}) async-start(f32[1,64,1,4,128]{4,3,2,0,1:T(4,128)} %get-tuple-element.74), calls=%async_computation.2 | async-start | bytes 262144 | tf_op jit(solution)/shard_map/all_to_all | solution.py:38
  73.9 1.8 %fusion.37 = f32[512,1024]{1,0:T(8,128)S(1)} fusion(s32[64,1024]{1,0:T(8,128)S(1)} %copy-done.2, f32[8,8,4,128]{3,2,1,0:T(4,128)S(1)} %bitcast.148), kind=kOutput, calls=%fused_computation.37 | convolution fusion | flops 402718720 | bytes 2490368 | tf_op jit(solution)/shard_map/dot_general | solution.py:94
  75.8 2.5 %fusion.18 = f32[64,512]{1,0:T(8,128)S(1)} fusion(f32[512,1024]{1,0:T(8,128)S(1)} %fusion.37, f32[512,1024]{1,0:T(8,128)S(1)} %copy-done.1, f32[1024]{0:T(1024)S(1)} %copy-done.5, s32[1024,64]{0,1:T(8,128)S(1)} %copy-done.3, f32[8,8,4,128]{3,2,1,0:T(4,128)S(1)} %bitcast.149, f32[8,8,4,128]{3,2,1,0:T(4,128)S(1)} %bitcast.137), kind=kOutput, calls=%fused_computation.16 | convolution fusion | flops 403963904 | bytes 4853760 | tf_op jit(solution)/shard_map/dot_general | solution.py:95
  79.1 10.0 %all_to_all.120 = f32[1,64,1,4,128]{4,3,2,0,1:T(4,128)S(1)} all-to-all(f32[1,64,1,4,128]{4,3,2,0,1:T(4,128)S(1)} %bitcast.158), channel_id=1, replica_groups=mesh['grp'=2,'gx'=4,'gy'=2,'row'=2] {'gx'}, dimensions={1} | all-to-all | bytes 262144 | tf_op jit(solution)/shard_map/all_to_all | solution.py:38
  91.8 1.4 %select_bitcast_fusion = f32[1,16,4,4,128]{4,3,1,0,2:T(4,128)} fusion(f32[16,4,4,128]{3,2,0,1:T(4,128)S(1)} %add.318, f32[16,4,4,128]{3,2,0,1:T(4,128)S(1)} %pad.146, f32[16,4,4,128]{3,2,0,1:T(4,128)S(1)} %pad.147, pred[4,128]{1,0:T(4,128)(4,1)} %get-tuple-element.75), kind=kLoop, calls=%fused_computation.91 | loop fusion | flops 65536 | bytes 524800 | tf_op jit(solution)/shard_map/stack | solution.py:41
  93.2 3.3 %all-to-all-start.7 = ((f32[1,16,4,4,128]{4,3,1,0,2:T(4,128)}), f32[1,16,4,4,128]{4,3,1,0,2:T(4,128)S(1)}, u32[]{:S(2)}, u32[]{:S(2)}) async-start(f32[1,16,4,4,128]{4,3,1,0,2:T(4,128)} %select_bitcast_fusion), calls=%async_computation.7 | async-start | bytes 262144 | tf_op jit(solution)/shard_map/all_to_all | solution.py:42
  99.8 2.6 %all-to-all-done.7 = f32[1,16,4,4,128]{4,3,1,0,2:T(4,128)S(1)} async-done(((f32[1,16,4,4,128]{4,3,1,0,2:T(4,128)}), f32[1,16,4,4,128]{4,3,1,0,2:T(4,128)S(1)}, u32[]{:S(2)}, u32[]{:S(2)}) %all-to-all-start.7) | async-done | bytes 131104 | tf_op jit(solution)/shard_map/all_to_all | solution.py:42
  102.4 3.3 %all-to-all-start.3 = ((f32[1,16,4,4,128]{4,3,1,0,2:T(4,128)}), f32[1,16,4,4,128]{4,3,1,0,2:T(4,128)S(1)}, u32[]{:S(2)}, u32[]{:S(2)}) async-start(f32[1,16,4,4,128]{4,3,1,0,2:T(4,128)} %select_bitcast_fusion.2), calls=%async_computation.3 | async-start | bytes 262144 | tf_op jit(solution)/shard_map/all_to_all | solution.py:42
  105.9 1.9 %collective-permute-start.6 = (f32[64,1,1,128]{3,2,0,1:T(1,128)S(1)}, f32[64,1,1,128]{3,2,0,1:T(1,128)S(1)}, u32[]{:S(2)}, u32[]{:S(2)}) collective-permute-start(f32[64,1,1,128]{3,2,0,1:T(1,128)S(1)} %get-tuple-element.15), channel_id=1, source_target_pairs={{1,0},{2,1},{3,2},{5,4},{6,5},{7,6},{9,8},{10,9},{11,10},{13,12},{... | collective-permute-start | bytes 98312 | tf_op jit(solution)/shard_map/ppermute | solution.py:22
  107.8 2.4 %collective-permute-start.7 = (f32[64,1,1,128]{3,2,0,1:T(1,128)S(1)}, f32[64,1,1,128]{3,2,0,1:T(1,128)S(1)}, u32[]{:S(2)}, u32[]{:S(2)}) collective-permute-start(f32[64,1,1,128]{3,2,0,1:T(1,128)S(1)} %get-tuple-element.14), channel_id=1, source_target_pairs={{0,1},{1,2},{2,3},{4,5},{5,6},{6,7},{8,9},{9,10},{10,11},{12,13},{... | collective-permute-start | bytes 98312 | tf_op jit(solution)/shard_map/ppermute | solution.py:19
  110.2 1.4 %all-to-all-done.3 = f32[1,16,4,4,128]{4,3,1,0,2:T(4,128)S(1)} async-done(((f32[1,16,4,4,128]{4,3,1,0,2:T(4,128)}), f32[1,16,4,4,128]{4,3,1,0,2:T(4,128)S(1)}, u32[]{:S(2)}, u32[]{:S(2)}) %all-to-all-start.3) | async-done | bytes 131104 | tf_op jit(solution)/shard_map/all_to_all | solution.py:42
  111.7 1.4 %collective-permute-done.7 = f32[64,1,1,128]{3,2,0,1:T(1,128)S(1)} collective-permute-done((f32[64,1,1,128]{3,2,0,1:T(1,128)S(1)}, f32[64,1,1,128]{3,2,0,1:T(1,128)S(1)}, u32[]{:S(2)}, u32[]{:S(2)}) %collective-permute-start.7) | collective-permute-done | bytes 32800 | tf_op jit(solution)/shard_map/ppermute | solution.py:19
  113.8 1.8 %fusion.35 = f32[512,1024]{1,0:T(8,128)S(1)} fusion(s32[64,1024]{1,0:T(8,128)S(1)} %copy-done.2, f32[8,8,4,128]{3,2,1,0:T(4,128)S(1)} %bitcast.150), kind=kOutput, calls=%fused_computation.35 | convolution fusion | flops 402718720 | bytes 2490368 | tf_op jit(solution)/shard_map/dot_general | solution.py:94
  115.6 2.5 %fusion.27 = f32[64,512]{1,0:T(8,128)S(1)} fusion(f32[512,1024]{1,0:T(8,128)S(1)} %fusion.35, f32[512,1024]{1,0:T(8,128)S(1)} %fusion.45, f32[1024]{0:T(1024)S(1)} %copy-done.5, s32[1024,64]{0,1:T(8,128)S(1)} %copy-done.3, f32[8,8,4,128]{3,2,1,0:T(4,128)S(1)} %bitcast.151, f32[8,8,4,128]{3,2,1,0:T(4,128)S(1)} %bitcast.143), kind=kOutput, calls=%fused_computation.19 | convolution fusion | flops 403963904 | bytes 4853760 | tf_op jit(solution)/shard_map/dot_general | solution.py:95
  (115 shorter events, 24.2 us)
Async XLA Ops:
  0.6 3.0 %copy-start.4 = (f32[64,1,4,128]{3,2,1,0:T(4,128)S(1)}, f32[64,1,4,128]{3,2,1,0:T(4,128)}, u32[]{:S(2)}) copy-start(f32[64,1,4,128]{3,2,1,0:T(4,128)} %param.7) | copy-start | bytes 393220
  0.6 3.0 %copy-start.5 = (f32[1024]{0:T(1024)S(1)}, f32[1024]{0:T(1024)}, u32[]{:S(2)}) copy-start(f32[1024]{0:T(1024)} %param.11) | copy-start | bytes 12292
  0.6 3.0 %copy-start.2 = (s32[64,1024]{1,0:T(8,128)S(1)}, s32[64,1024]{1,0:T(8,128)}, u32[]{:S(2)}) copy-start(s32[64,1024]{1,0:T(8,128)} %param.13) | copy-start | bytes 786436
  3.6 11.7 %copy-start.13 = (f32[4,128]{1,0:T(4,128)S(1)}, f32[4,128]{1,0:T(4,128)}, u32[]{:S(2)}) copy-start(f32[4,128]{1,0:T(4,128)} %param.9) | copy-start | bytes 6148
  3.6 21.0 %copy-start.12 = (s32[4,128]{1,0:T(4,128)S(1)}, s32[4,128]{1,0:T(4,128)}, u32[]{:S(2)}) copy-start(s32[4,128]{1,0:T(4,128)} %param.10) | copy-start | bytes 6148
  6.1 9.3 %collective-permute-start = (f32[64,1,1,128]{3,2,0,1:T(1,128)S(1)}, f32[64,1,1,128]{3,2,0,1:T(1,128)S(1)}, u32[]{:S(2)}, u32[]{:S(2)}) collective-permute-start(f32[64,1,1,128]{3,2,0,1:T(1,128)S(1)} %get-tuple-element.49), channel_id=1, source_target_pairs={{1,0},{2,1},{3,2},{5,4},{6,5},{7,6},{9,8},{10,9},{11,10},{13,12},{... | collective-permute-start | bytes 98312 | tf_op jit(solution)/shard_map/ppermute | solution.py:22
  8.0 7.4 %collective-permute-start.1 = (f32[64,1,1,128]{3,2,0,1:T(1,128)S(1)}, f32[64,1,1,128]{3,2,0,1:T(1,128)S(1)}, u32[]{:S(2)}, u32[]{:S(2)}) collective-permute-start(f32[64,1,1,128]{3,2,0,1:T(1,128)S(1)} %get-tuple-element.48), channel_id=1, source_target_pairs={{0,1},{1,2},{2,3},{4,5},{5,6},{6,7},{8,9},{9,10},{10,11},{12,13},{... | collective-permute-start | bytes 98312 | tf_op jit(solution)/shard_map/ppermute | solution.py:19
  10.5 10.8 %all-to-all-start.4 = ((f32[1,64,1,4,128]{4,3,2,0,1:T(4,128)}), f32[1,64,1,4,128]{4,3,2,0,1:T(4,128)S(1)}, u32[]{:S(2)}, u32[]{:S(2)}) async-start(f32[1,64,1,4,128]{4,3,2,0,1:T(4,128)} %bitcast.26), calls=%async_computation.4 | async-start | bytes 262144 | tf_op jit(solution)/shard_map/all_to_all | solution.py:38
  15.3 15.3 %copy-start.8 = (f32[4,128]{1,0:T(4,128)}, f32[4,128]{1,0:T(4,128)S(1)}, u32[]{:S(2)}) copy-start(f32[4,128]{1,0:T(4,128)S(1)} %get-tuple-element.82) | copy-start | bytes 6148
  15.4 15.2 %copy-start.6 = (f32[2,4,128]{2,1,0:T(4,128)}, f32[2,4,128]{2,1,0:T(4,128)S(1)}, u32[]{:S(2)}) copy-start(f32[2,4,128]{2,1,0:T(4,128)S(1)} %reverse_bitcast_fusion) | copy-start | bytes 12292
  21.2 9.2 %all-to-all-start = ((f32[1,64,1,4,128]{4,3,2,0,1:T(4,128)}), f32[1,64,1,4,128]{4,3,2,0,1:T(4,128)S(1)}, u32[]{:S(2)}, u32[]{:S(2)}) async-start(f32[1,64,1,4,128]{4,3,2,0,1:T(4,128)} %fusion.69), calls=%async_computation | async-start | bytes 262144 | tf_op jit(solution)/shard_map/all_to_all | solution.py:38
  31.9 15.7 %copy-start.3 = (s32[1024,64]{0,1:T(8,128)S(1)}, s32[1024,64]{0,1:T(8,128)}, u32[]{:S(2)}) copy-start(s32[1024,64]{0,1:T(8,128)} %param.12) | copy-start | bytes 786436
  34.5 9.2 %all-to-all-start.1 = ((f32[1,16,4,4,128]{4,3,1,0,2:T(4,128)}), f32[1,16,4,4,128]{4,3,1,0,2:T(4,128)S(1)}, u32[]{:S(2)}, u32[]{:S(2)}) async-start(f32[1,16,4,4,128]{4,3,1,0,2:T(4,128)} %select_bitcast_fusion.3), calls=%async_computation.1 | async-start | bytes 262144 | tf_op jit(solution)/shard_map/all_to_all | solution.py:42
  43.7 18.0 %all-to-all-start.5 = ((f32[1,16,4,4,128]{4,3,1,0,2:T(4,128)}), f32[1,16,4,4,128]{4,3,1,0,2:T(4,128)S(1)}, u32[]{:S(2)}, u32[]{:S(2)}) async-start(f32[1,16,4,4,128]{4,3,1,0,2:T(4,128)} %select_bitcast_fusion.1), calls=%async_computation.5 | async-start | bytes 262144 | tf_op jit(solution)/shard_map/all_to_all | solution.py:42
  49.4 1.3 %copy-start = (f32[512,1024]{1,0:T(8,128)}, f32[512,1024]{1,0:T(8,128)S(1)}, u32[]{:S(2)}) copy-start(f32[512,1024]{1,0:T(8,128)S(1)} %fusion.43) | copy-start | bytes 6291460
  50.8 10.9 %copy-start.9 = (f32[4,128]{1,0:T(4,128)S(1)}, f32[4,128]{1,0:T(4,128)}, u32[]{:S(2)}) copy-start(f32[4,128]{1,0:T(4,128)} %copy-done.8) | copy-start | bytes 6148
  53.2 4.3 %collective-permute-start.2 = (f32[64,1,1,128]{3,2,0,1:T(1,128)S(1)}, f32[64,1,1,128]{3,2,0,1:T(1,128)S(1)}, u32[]{:S(2)}, u32[]{:S(2)}) collective-permute-start(f32[64,1,1,128]{3,2,0,1:T(1,128)S(1)} %get-tuple-element.40), channel_id=1, source_target_pairs={{1,0},{2,1},{3,2},{5,4},{6,5},{7,6},{9,8},{10,9},{11,10},{13,12},{... | collective-permute-start | bytes 98312 | tf_op jit(solution)/shard_map/ppermute | solution.py:22
  55.1 5.3 %collective-permute-start.3 = (f32[64,1,1,128]{3,2,0,1:T(1,128)S(1)}, f32[64,1,1,128]{3,2,0,1:T(1,128)S(1)}, u32[]{:S(2)}, u32[]{:S(2)}) collective-permute-start(f32[64,1,1,128]{3,2,0,1:T(1,128)S(1)} %get-tuple-element.39), channel_id=1, source_target_pairs={{0,1},{1,2},{2,3},{4,5},{5,6},{6,7},{8,9},{9,10},{10,11},{12,13},{... | collective-permute-start | bytes 98312 | tf_op jit(solution)/shard_map/ppermute | solution.py:19
  63.8 9.4 %collective-permute-start.4 = (f32[64,1,1,128]{3,2,0,1:T(1,128)S(1)}, f32[64,1,1,128]{3,2,0,1:T(1,128)S(1)}, u32[]{:S(2)}, u32[]{:S(2)}) collective-permute-start(f32[64,1,1,128]{3,2,0,1:T(1,128)S(1)} %get-tuple-element.24), channel_id=1, source_target_pairs={{1,0},{2,1},{3,2},{5,4},{6,5},{7,6},{9,8},{10,9},{11,10},{13,12},{... | collective-permute-start | bytes 98312 | tf_op jit(solution)/shard_map/ppermute | solution.py:22
  65.7 7.5 %collective-permute-start.5 = (f32[64,1,1,128]{3,2,0,1:T(1,128)S(1)}, f32[64,1,1,128]{3,2,0,1:T(1,128)S(1)}, u32[]{:S(2)}, u32[]{:S(2)}) collective-permute-start(f32[64,1,1,128]{3,2,0,1:T(1,128)S(1)} %get-tuple-element.23), channel_id=1, source_target_pairs={{0,1},{1,2},{2,3},{4,5},{5,6},{6,7},{8,9},{9,10},{10,11},{12,13},{... | collective-permute-start | bytes 98312 | tf_op jit(solution)/shard_map/ppermute | solution.py:19
  68.1 11.0 %all-to-all-start.2 = ((f32[1,64,1,4,128]{4,3,2,0,1:T(4,128)}), f32[1,64,1,4,128]{4,3,2,0,1:T(4,128)S(1)}, u32[]{:S(2)}, u32[]{:S(2)}) async-start(f32[1,64,1,4,128]{4,3,2,0,1:T(4,128)} %get-tuple-element.74), calls=%async_computation.2 | async-start | bytes 262144 | tf_op jit(solution)/shard_map/all_to_all | solution.py:38
  73.2 2.6 %copy-start.1 = (f32[512,1024]{1,0:T(8,128)S(1)}, f32[512,1024]{1,0:T(8,128)}, u32[]{:S(2)}) copy-start(f32[512,1024]{1,0:T(8,128)} %copy-done) | copy-start | bytes 6291460
  75.8 13.4 %copy-start.7 = (f32[2,4,128]{2,1,0:T(4,128)S(1)}, f32[2,4,128]{2,1,0:T(4,128)}, u32[]{:S(2)}) copy-start(f32[2,4,128]{2,1,0:T(4,128)} %copy-done.6) | copy-start | bytes 12292
  90.1 9.0 %copy-start.11 = (pred[4,128]{1,0:T(4,128)(4,1)S(1)}, pred[4,128]{1,0:T(4,128)(4,1)}, u32[]{:S(2)}) copy-start(pred[4,128]{1,0:T(4,128)(4,1)} %get-tuple-element.76) | copy-start | bytes 1540
  90.5 15.2 %copy-start.10 = (f32[4,128]{1,0:T(4,128)S(1)}, f32[4,128]{1,0:T(4,128)}, u32[]{:S(2)}) copy-start(f32[4,128]{1,0:T(4,128)} %copy-done.8) | copy-start | bytes 6148
  93.2 9.2 %all-to-all-start.7 = ((f32[1,16,4,4,128]{4,3,1,0,2:T(4,128)}), f32[1,16,4,4,128]{4,3,1,0,2:T(4,128)S(1)}, u32[]{:S(2)}, u32[]{:S(2)}) async-start(f32[1,16,4,4,128]{4,3,1,0,2:T(4,128)} %select_bitcast_fusion), calls=%async_computation.7 | async-start | bytes 262144 | tf_op jit(solution)/shard_map/all_to_all | solution.py:42
  102.4 9.2 %all-to-all-start.3 = ((f32[1,16,4,4,128]{4,3,1,0,2:T(4,128)}), f32[1,16,4,4,128]{4,3,1,0,2:T(4,128)S(1)}, u32[]{:S(2)}, u32[]{:S(2)}) async-start(f32[1,16,4,4,128]{4,3,1,0,2:T(4,128)} %select_bitcast_fusion.2), calls=%async_computation.3 | async-start | bytes 262144 | tf_op jit(solution)/shard_map/all_to_all | solution.py:42
  105.9 5.8 %collective-permute-start.6 = (f32[64,1,1,128]{3,2,0,1:T(1,128)S(1)}, f32[64,1,1,128]{3,2,0,1:T(1,128)S(1)}, u32[]{:S(2)}, u32[]{:S(2)}) collective-permute-start(f32[64,1,1,128]{3,2,0,1:T(1,128)S(1)} %get-tuple-element.15), channel_id=1, source_target_pairs={{1,0},{2,1},{3,2},{5,4},{6,5},{7,6},{9,8},{10,9},{11,10},{13,12},{... | collective-permute-start | bytes 98312 | tf_op jit(solution)/shard_map/ppermute | solution.py:22
  107.8 5.2 %collective-permute-start.7 = (f32[64,1,1,128]{3,2,0,1:T(1,128)S(1)}, f32[64,1,1,128]{3,2,0,1:T(1,128)S(1)}, u32[]{:S(2)}, u32[]{:S(2)}) collective-permute-start(f32[64,1,1,128]{3,2,0,1:T(1,128)S(1)} %get-tuple-element.14), channel_id=1, source_target_pairs={{0,1},{1,2},{2,3},{4,5},{5,6},{6,7},{8,9},{9,10},{10,11},{12,13},{... | collective-permute-start | bytes 98312 | tf_op jit(solution)/shard_map/ppermute | solution.py:19
where the time goes:
time: 121 us; the launch traced here: 119 us
  starting transfers between devices  44.4 us (37%)
  waiting for transfers between devices  20.1 us (17%)
  matrix products  18.1 us (15%)
  other arithmetic  15.8 us (13%)
  blocking collectives  10 us (8%)
  local copies, waits for them, and re-layouts  9.79 us (8%)
  between operations  1.28 us (1%)
    all_to_all x4, starting transfers between devices, sweep_fields(): lax.all_to_all(results, 'gx', split_axis=2, concat_axis=1, tiled=True)  13.8 us
    all_to_all x3, starting transfers between devices, sweep_fields(): lax.all_to_all(stacked, 'gx', split_axis=1, concat_axis=2, tiled=True)  13.3 us
    all_to_all x3, waiting for transfers between devices, sweep_fields(): lax.all_to_all(stacked, 'gx', split_axis=1, concat_axis=2, tiled=True)  10.5 us
    all_to_all x1, blocking collectives, sweep_fields(): lax.all_to_all(stacked, 'gx', split_axis=1, concat_axis=2, tiled=True)  10 us
    ppermute x4, starting transfers between devices, padded_2(): lax.ppermute(lax.slice_in_dim(block, block.shape[dim] - width, None, axis...  9.61 us
    ppermute x4, starting transfers between devices, padded_2(): lax.ppermute(lax.slice_in_dim(block, 0, width, axis=dim), axis, backward)  7.68 us
    pad x16, local copies, waits for them, and re-layouts, recurrence(): lax.associative_scan(combine_pairs, (multipliers, values), reverse=backwa...  6.68 us
    all_to_all x4, waiting for transfers between devices, sweep_fields(): lax.all_to_all(results, 'gx', split_axis=2, concat_axis=1, tiled=True)  5.31 us
  transfers between devices with their start and end apart: 15, of which 8 were waited for; matrix products, arithmetic and copies ran while one was open for 17% of the time, Pallas kernels for 0%

commit v1 on v0

v1 whole, which is shorter than its diff:
```python
import functools
import jax
import jax.numpy as jnp
from jax import lax
from jax.experimental import pallas as pl
from jax.experimental.pallas import tpu as pltpu
from jax.sharding import PartitionSpec as P

STEPS = 2
LANES = 128

time_step = 0.1
diffusion = 0.1
highest = lax.Precision.HIGHEST
f32 = jnp.float32
bf16 = jnp.bfloat16


def padded_2(block, sides, width):
    for axis, dim in sides:
        count = lax.axis_size(axis)
        forward = [(i, i + 1) for i in range(count - 1)]
        backward = [(target, source) for source, target in forward]
        low = lax.ppermute(
            lax.slice_in_dim(block, block.shape[dim] - width, None, axis=dim), axis, forward
        )
        high = lax.ppermute(lax.slice_in_dim(block, 0, width, axis=dim), axis, backward)
        block = jnp.concatenate([low, block, high], axis=dim)
    return block


def combine_pairs(leading, trailing):
    return (leading[0] * trailing[0], trailing[0] * leading[1] + trailing[1])


def recurrence(values, weight, backward):
    multipliers = jnp.broadcast_to(weight[None, None], (1, values.shape[1]) + weight.shape)
    return lax.associative_scan(combine_pairs, (multipliers, values), reverse=backward, axis=1)


def sweep(values, weight, upward):
    pencils = lax.all_to_all(values, "gx", split_axis=0, concat_axis=1, tiled=True)
    rising = recurrence(pencils, weight, False)[1]
    falling = recurrence(pencils, weight, True)[1]
    result = jnp.where(upward[None, None], rising, falling)
    return lax.all_to_all(result, "gx", split_axis=1, concat_axis=0, tiled=True)


def smooth(values):
    padded = padded_2(values, ((("gy", "row"), 2),), 1)
    padded = jnp.pad(padded, [(0, 0)] * (padded.ndim - 1) + [(1, 1)])
    beside_all = (
        padded[..., 2:, 1:-1]
        + padded[..., :-2, 1:-1]
        + padded[..., 1:-1, 2:]
        + padded[..., 1:-1, :-2]
    )
    return values + diffusion * (beside_all - 4.0 * values)


def reaction_rates(cells, order_float, rate_const):
    activity = 0.5 * jnp.log1p(cells * cells)
    return rate_const[:, None] * jnp.exp(jnp.dot(order_float, activity, precision=highest))


def per_slice(function, arrays, shape):
    flats = [item.reshape(shape[0], -1) for item in arrays]
    return function(*flats).reshape(shape)


def general(conc, cotangent, courant, direction, rate_const, orders, stoich):
    order_float = orders.astype(f32)
    stoich_float = stoich.astype(f32)
    order_trans = order_float.T
    stoich_trans = stoich_float.T
    retain = courant / (1.0 + courant)
    admit = 1.0 / (1.0 + courant)

    def react(cells):
        return cells + time_step * jnp.dot(
            stoich_float, reaction_rates(cells, order_float, rate_const), precision=highest
        )

    def react_back(cells, spread):
        rates = reaction_rates(cells, order_float, rate_const)
        pulled = jnp.dot(stoich_trans, spread, precision=highest)
        summed = jnp.dot(order_trans, rates * pulled, precision=highest)
        return spread + time_step * cells / (1.0 + cells * cells) * summed

    states = [conc]
    for position in range(STEPS):
        current = states[-1]
        starred = per_slice(react, [current], current.shape)
        states.append(sweep(admit * smooth(starred), retain, direction == 1))
    adjoint = cotangent
    for position in reversed(range(STEPS)):
        carried = admit * sweep(adjoint, retain, direction == 0)
        spread = smooth(carried)
        adjoint = per_slice(react_back, [states[position], spread], spread.shape)
    return (states[-1], adjoint)


def split(values):
    high = values.astype(bf16)
    return high, (values - high.astype(f32)).astype(bf16)


def stacked(values):
    high, low = split(values)
    return jnp.concatenate([high, low], axis=0)


def mul(left, right):
    return jnp.dot(left, right, preferred_element_type=f32)


def exponent_input(cells):
    return stacked((0.5 * 1.4426950408889634) * jnp.log(1.0 + cells * cells))


def scaled(left, rate_const):
    return stacked(left * rate_const)


def product(left, values):
    species = left.shape[0] // 2
    high, low = split(values)
    both = mul(left, high)
    return both[:species] + both[species:] + mul(left[:species], low)


def lane_iota(rows):
    return lax.broadcasted_iota(jnp.int32, (rows, LANES), 1)


class Plan:
    def __init__(self, species, rows, depth, parts):
        self.species, self.rows, self.depth, self.parts = species, rows, depth, parts
        self.halo = STEPS
        self.cut = depth // parts
        self.width = self.cut + 2 * self.halo
        self.own = rows * self.width
        self.tail = self.own - LANES
        self.groups = LANES // self.tail if self.tail > 0 and LANES % self.tail == 0 else 0
        need = (rows + 2 * self.halo) * self.width
        self.lanes = -(-need // LANES) * LANES
        need = (rows + 2 * self.halo - 2) * self.width
        self.inner = -(-need // LANES) * LANES


def fits(mesh, conc):
    parts = mesh.shape["gx"]
    species, length, across, depth = conc
    rows = across // (mesh.shape["gy"] * mesh.shape["row"])
    if mesh.shape["row"] != 2 or length != mesh.shape["grp"] * parts or depth != LANES:
        return False
    if depth % parts or parts not in (2, 4, 8) or rows != parts or STEPS != 2:
        return False
    plan = Plan(species, rows, depth, parts)
    if plan.groups == 0 or (2 * species) % (8 * plan.groups) or species % 16:
        return False
    if (rows - 1) * plan.width >= LANES or plan.tail + 2 * plan.width > LANES:
        return False
    return plan.lanes >= 3 * LANES


def window(pieces, target, plan):
    count = pieces[0].shape[0]
    lane = lane_iota(count)
    main = jnp.zeros((count, LANES), f32)
    tail = None
    for row in range(plan.rows):
        first = plan.width * row
        shift = first - (plan.cut * target - plan.halo)
        rolled = pltpu.roll(pieces[row], shift % LANES, 1)
        low = first + (plan.halo if target == 0 else 0)
        high = first + plan.width - (plan.halo if target == plan.parts - 1 else 0)
        main = jnp.where((lane >= low) & (lane < high), rolled, main)
        if row == plan.rows - 1:
            tail = jnp.where(lane < high - LANES, rolled, 0.0)
    return main, tail


def pack_tail(tail, plan):
    rows = tail.shape[0] // plan.groups
    lane = lane_iota(rows)
    packed = tail[:rows]
    for group in range(1, plan.groups):
        moved = pltpu.roll(tail[rows * group : rows * (group + 1)], plan.tail * group, 1)
        packed = jnp.where(lane >= plan.tail * group, moved, packed)
    return packed


def unpack_tail(packed, plan):
    lane = lane_iota(packed.shape[0])
    parts = [packed]
    for group in range(1, plan.groups):
        parts.append(pltpu.roll(packed, LANES - plan.tail * group, 1))
    return jnp.concatenate([jnp.where(lane < plan.tail, part, 0.0) for part in parts], axis=0)


def first_kernel(plan, conc, cot, cour, direct, rate, orders, stoich, own, columns, *rest):
    sends, pieces = rest[:-1], rest[-1]
    species, rows, parts = plan.species, plan.rows, plan.parts
    flip = lax.axis_index("row") == 1
    me = lax.axis_index("gx")
    order_float = orders[...].astype(f32)
    left = jnp.concatenate([order_float, order_float], axis=1).astype(bf16)
    right = scaled(stoich[...].astype(f32), rate[...])
    stars = []
    half = 2 * LANES
    per = half // LANES
    loaded = [conc[pl.ds(row, species, stride=rows), :] for row in range(rows)]
    for start in range(0, rows, per):
        cells = jnp.concatenate(loaded[start : start + per], axis=1)
        growth = jnp.exp2(mul(left, exponent_input(cells)))
        star = cells + time_step * product(right, growth)
        stars += [star[:, LANES * n : LANES * (n + 1)] for n in range(per)]
    costate = [cot[pl.ds(row, species, stride=rows), :] for row in range(rows)]
    both = [jnp.concatenate([stars[row], costate[row]], axis=0) for row in range(rows)]
    both = [jnp.where(flip, both[rows - 1 - row], both[row]) for row in range(rows)]
    sublane = lax.broadcasted_iota(jnp.int32, (8, LANES), 0)
    facts = []
    for row in range(rows):
        a = jnp.where(flip, cour[rows - 1 - row : rows - row, :], cour[row : row + 1, :])
        b = jnp.where(flip, direct[rows - 1 - row : rows - row, :], direct[row : row + 1, :])
        fact = jnp.where(sublane == 0, a, jnp.where(sublane == 1, b.astype(f32), 1.0))
        facts.append(fact)
    size = 2 * species
    small = size // plan.groups
    for target in range(parts):
        main, tail = window(both, target, plan)
        pieces[target, :size, :] = main
        pieces[target, size : size + small, :] = pack_tail(tail, plan)
        main, tail = window(facts, target, plan)
        pieces[target, size + small : size + small + 8, :] = main
        pieces[target, size + small + 8 : size + small + 16, :] = tail
    own[...] = pieces[me, : size + small, :]
    columns[:, :LANES] = pieces[me, size + small : size + small + 8, :]
    columns[:, LANES:] = pieces[me, size + small + 8 : size + small + 16, :]
    for step, send in enumerate(sends, 1):
        send[...] = pieces[me ^ step, : size + small, :]


def gather_planes(plan, planes, own, received):
    me = lax.axis_index("gx")
    planes[me] = own[...]
    for step, block in enumerate(received, 1):
        planes[me ^ step] = block[...]


def halo_kernel(plan, *refs):
    parts, size = plan.parts, 2 * plan.species
    own, received, columns = refs[0], refs[1:parts], refs[parts]
    inner, outer, planes = refs[parts + 1 :]
    gather_planes(plan, planes, own, received)

    def put(where, count, main, tail):
        outer[where : where + count, :] = main
        lane = lane_iota(count)
        last = (plan.rows - 1) * plan.width
        near = pltpu.roll(main, LANES - last, 1)
        wrapped = pltpu.roll(tail, LANES - last, 1)
        near = jnp.where(lane < LANES - last, near, wrapped)
        far = pltpu.roll(main, (plan.width - last + plan.width) % LANES, 1)
        near = jnp.where(lane < plan.width, near, far)
        inner[where : where + count, :] = near

    small = size // plan.groups
    for plane in range(parts):
        put(plane * size, size, planes[plane, :size, :], unpack_tail(planes[plane, size : size + small, :], plan))
    put(parts * size, 8, columns[:, :LANES], columns[:, LANES:])


def turn(values, amount):
    return pltpu.roll(values, amount % values.shape[1], 1)


def smoothed(values, width):
    beside = turn(values, 1) + turn(values, -1) + turn(values, width) + turn(values, -width)
    return values + diffusion * (beside - 4.0 * values)


def swept(planes, retain, upward):
    count = len(planes)
    rising, falling = [planes[0]], [planes[-1]]
    for n in range(1, count):
        rising.append(retain * rising[-1] + planes[n])
        falling.append(retain * falling[-1] + planes[count - 1 - n])
    falling.reverse()
    return [jnp.where(upward, a, b) for a, b in zip(rising, falling)]


def middle_kernel(plan, *refs):
    parts, species = plan.parts, plan.species
    size = 2 * species
    own, received, columns = refs[0], refs[1:parts], refs[parts]
    inner, outer, left_ref, right_ref, pull_ref, push_ref = refs[parts + 1 : parts + 7]
    results, planes = refs[parts + 7 : -1], refs[-1]
    gather_planes(plan, planes, own, received)
    width, full, part = plan.width, plan.lanes, plan.inner
    small = size // plan.groups

    def whole(main, tail, near, far):
        count = main.shape[0]
        lane = lane_iota(count)
        used = 2 * width
        second = jnp.where((lane >= plan.tail) & (lane < plan.tail + used), pltpu.roll(near, plan.tail, 1), tail)
        last = jnp.where(lane >= LANES - width, pltpu.roll(far, LANES - width, 1), 0.0)
        before = pltpu.roll(far, (LANES - 3 * width) % LANES, 1)
        last = jnp.where((lane >= LANES - 2 * width) & (lane < LANES - width), before, last)
        blocks = [main, second]
        blocks += [jnp.zeros_like(main)] * (full // LANES - 3)
        return jnp.concatenate(blocks + [last], axis=1)

    facts = whole(columns[:, :LANES], columns[:, LANES:], inner[parts * size :, :], outer[parts * size :, :])
    cour = facts[0:1, :]
    admit = 1.0 / (1.0 + cour)
    retain = cour / (1.0 + cour)
    upward = facts[1:2, :] > 0.5
    downward = facts[1:2, :] < 0.5
    inside = facts[2:3, :]

    def cropped(values):
        return turn(values, width)[:, :part]

    states, costates = [], []
    for plane in range(parts):
        rows = slice(plane * size, (plane + 1) * size)
        tail = unpack_tail(planes[plane, size : size + small, :], plan)
        both = whole(planes[plane, :size, :], tail, inner[rows, :], outer[rows, :])
        states.append(admit * smoothed(both[:species], width))
        costates.append(both[species:])
    states = [cropped(v) for v in swept(states, retain, upward)]
    costates = [admit * v for v in swept(costates, retain, downward)]
    costates = [cropped(smoothed(v, width)) for v in costates]
    admit, retain = cropped(admit), cropped(retain)
    inside = cropped(inside) > 0.5
    upward = cropped(facts[1:2, :]) > 0.5
    downward = cropped(facts[1:2, :]) < 0.5
    left, right, pull, push = left_ref[...], right_ref[...], pull_ref[...], push_ref[...]
    stars, backs = [], []
    for plane in range(parts):
        cells, spread = states[plane], costates[plane]
        growth = jnp.exp2(mul(left, exponent_input(cells)))
        star = cells + time_step * product(right, growth)
        stars.append(jnp.where(inside, star, 0.0))
        summed = product(push, growth * mul(pull, stacked(spread)))
        back = spread + time_step * cells / (1.0 + cells * cells) * summed
        backs.append(jnp.where(inside, back, 0.0))
    final = swept([admit * smoothed(v, width) for v in stars], retain, upward)
    spreads = [admit * v for v in swept(backs, retain, downward)]
    spreads = [smoothed(v, width) for v in spreads]

    def dense(values):
        lane = lane_iota(values.shape[0])
        out = None
        for row in range(plan.rows):
            moved = turn(values, plan.cut * row - (width * (row + 1) + plan.halo))[:, :LANES]
            out = moved if row == 0 else jnp.where(lane >= plan.cut * row, moved, out)
        return out

    for plane in range(parts):
        planes[plane, :species, :] = dense(final[plane])
        planes[plane, species:size, :] = dense(spreads[plane])
    me = lax.axis_index("gx")
    for step, result in enumerate(results):
        result[...] = planes[me ^ step, :size, :]


def last_kernel(plan, *refs):
    parts, species, rows = plan.parts, plan.species, plan.rows
    size = 2 * species
    own, received = refs[0], refs[1:parts]
    conc, left_ref, pull_ref, push_ref = refs[parts : parts + 4]
    final, adjoint, planes = refs[parts + 4 :]
    gather_planes(plan, planes, own, received)
    flip = lax.axis_index("row") == 1
    lane = lane_iota(size)
    blocks = []
    for row in range(rows):
        out = None
        for piece in range(parts):
            moved = pltpu.roll(planes[piece, :, :], (plan.cut * (piece - row)) % LANES, 1)
            out = moved if piece == 0 else jnp.where(lane >= plan.cut * piece, moved, out)
        blocks.append(out)
    blocks = [jnp.where(flip, blocks[rows - 1 - row], blocks[row]) for row in range(rows)]
    for row in range(rows):
        final[pl.ds(row, species, stride=rows), :] = blocks[row][:species]
    left, pull, push = left_ref[...], pull_ref[...], push_ref[...]
    per = 2
    for start in range(0, rows, per):
        cells = jnp.concatenate([conc[pl.ds(start + n, species, stride=rows), :] for n in range(per)], axis=1)
        spread = jnp.concatenate([blocks[start + n][species:] for n in range(per)], axis=1)
        growth = jnp.exp2(mul(left, exponent_input(cells)))
        summed = product(push, growth * mul(pull, stacked(spread)))
        back = spread + time_step * cells / (1.0 + cells * cells) * summed
        for n in range(per):
            adjoint[pl.ds(start + n, species, stride=rows), :] = back[:, LANES * n : LANES * (n + 1)]


def tables_kernel(rate, orders, stoich, own, left, right, pull, push):
    order_float = orders[...].astype(f32)
    stoich_float = stoich[...].astype(f32)
    left[...] = jnp.concatenate([order_float, order_float], axis=1).astype(bf16)
    right[...] = scaled(stoich_float, rate[...])
    turned = stoich_float.T
    pull[...] = jnp.concatenate([turned, turned], axis=1).astype(bf16)
    push[...] = scaled(order_float.T, rate[...])


def call(kernel, outs, scratch=(), flops=0):
    return pl.pallas_call(
        kernel,
        out_shape=outs,
        scratch_shapes=scratch,
        compiler_params=pltpu.CompilerParams(vmem_limit_bytes=32 * 1024 * 1024),
        cost_estimate=pl.CostEstimate(flops=flops, bytes_accessed=1 << 20, transcendentals=0),
    )


def columns_path(plan, gy, conc, cotangent, courant, direction, rate_const, orders, stoich):
    species, rows, parts = plan.species, plan.rows, plan.parts
    size = 2 * species
    shape = conc.shape
    count = rate_const.shape[0]
    rate = rate_const.reshape(1, count)
    flat = conc.reshape(species * rows, LANES)
    height = size + size // plan.groups
    block = jax.ShapeDtypeStruct((height, LANES), f32)
    own, columns, *sends = call(
        functools.partial(first_kernel, plan),
        [block, jax.ShapeDtypeStruct((8, 2 * LANES), f32)] + [block] * (parts - 1),
        [pltpu.VMEM((parts, height + 16, LANES), f32)],
        flops=1 << 28,
    )(flat, cotangent.reshape(species * rows, LANES), courant, direction, rate, orders, stoich)
    pairs = [[(i, i ^ step) for i in range(parts)] for step in range(1, parts)]
    received = [lax.ppermute(send, "gx", pair) for send, pair in zip(sends, pairs)]
    left, right, pull, push = call(
        tables_kernel,
        [
            jax.ShapeDtypeStruct((count, size), bf16),
            jax.ShapeDtypeStruct((size, count), bf16),
            jax.ShapeDtypeStruct((count, size), bf16),
            jax.ShapeDtypeStruct((size, count), bf16),
        ],
        flops=1 << 26,
    )(rate, orders, stoich, own)
    planes = pltpu.VMEM((parts, height, LANES), f32)
    edge = jax.ShapeDtypeStruct((parts * size + 8, LANES), f32)
    inner, outer = call(functools.partial(halo_kernel, plan), [edge, edge], [planes], flops=1 << 26)(
        own, *received, columns
    )
    cross = [(2 * n + 1, 2 * n + 2) for n in range(gy - 1)]
    outer = lax.ppermute(outer, ("gy", "row"), cross + [(b, a) for a, b in cross])
    inner = lax.ppermute(inner, "row", [(0, 1), (1, 0)])
    out = jax.ShapeDtypeStruct((size, LANES), f32)
    own, *sends = call(functools.partial(middle_kernel, plan), [out] * parts, [planes], flops=1 << 29)(
        own, *received, columns, inner, outer, left, right, pull, push
    )
    received = [lax.ppermute(send, "gx", pair) for send, pair in zip(sends, pairs)]
    result = jax.ShapeDtypeStruct((species * rows, LANES), f32)
    final, adjoint = call(
        functools.partial(last_kernel, plan),
        [result, result],
        [pltpu.VMEM((parts, size, LANES), f32)],
        flops=1 << 28,
    )(own, *received, flat, left, pull, push)
    return final.reshape(shape), adjoint.reshape(shape)


def solution(mesh):
    placed = (
        P(None, ("grp", "gx"), ("gy", "row"), None),
        P(None, ("grp", "gx"), ("gy", "row"), None),
        P(("grp", "gy", "row"), None),
        P(("grp", "gy", "row"), None),
        P(),
        P(),
        P(),
    )

    def program(*arrays):
        shape = arrays[0].shape
        if fits(mesh, shape):
            rows = shape[2] // (mesh.shape["gy"] * mesh.shape["row"])
            plan = Plan(shape[0], rows, shape[3], mesh.shape["gx"])
            body = functools.partial(columns_path, plan, mesh.shape["gy"])
        else:
            body = general
        return jax.shard_map(
            body,
            mesh=mesh,
            in_specs=placed,
            out_specs=placed[:2],
            check_vma=False,
        )(*arrays)

    return program
```

time: 121 us -> 38.3 us (0.32); the launches traced: 119 us -> 38.1 us
  starting transfers between devices: 44.4 us -> 11.5 us
  matrix products: 18.1 us -> 0 us
  other arithmetic: 15.8 us -> 0 us
  blocking collectives: 10 us -> 0 us
  Pallas kernels: 0 us -> 8.73 us
  local copies, waits for them, and re-layouts: 9.79 us -> 1.85 us
  waiting for transfers between devices: 20.1 us -> 15.2 us
    all_to_all x7 -> x0, starting transfers between devices: 27.1 us -> none  [the longest x4 13.8 us: sweep_fields(): lax.all_to_all(results, 'gx', split_axis=2, concat_axis=1, tiled=True)]
    dot_general x8 -> x0, matrix products: 18.1 us -> none  [the longest x2 4.91 us: react_back(): summed = jnp.dot(order_trans, rates * pulled, precision=highest)]
    all_to_all x7 -> x0, waiting for transfers between devices: 15.8 us -> none  [the longest x3 10.5 us: sweep_fields(): lax.all_to_all(stacked, 'gx', split_axis=1, concat_axis=2, tiled=True)]
    ppermute x8, waiting for transfers between devices: 4.24 us -> 15.2 us  [the longest x6 10.5 us: columns_path(): lax.ppermute(send, 'gx', pair)]
    all_to_all x1 -> x0, blocking collectives: 10 us -> none  [sweep_fields(): lax.all_to_all(stacked, 'gx', split_axis=1, concat_axis=2, tiled=True)]
    pallas_call x0 -> x5, Pallas kernels: none -> 8.73 us  [the longest x1 4.39 us: columns_path(): call(functools.partial(middle_kernel, plan), [out] * parts, [planes], flo...]
    pad x16 -> x0, local copies, waits for them, and re-layouts: 6.68 us -> none  [recurrence(): lax.associative_scan(combine_pairs, (multipliers, values), reverse=backwa...]
    ppermute x8, starting transfers between devices: 17.3 us -> 11.5 us  [the longest x6 8.9 us: columns_path(): lax.ppermute(send, 'gx', pair)]
  transfers between devices with their start and end apart: 15 -> 8, of which waited for: 8 -> 5; matrix products, arithmetic and copies ran while one was open for 17% -> 0% of each run, Pallas kernels for 0% -> 1%
where the time goes in v1:
time: 38.3 us; the launch traced here: 38.1 us
  waiting for transfers between devices  15.2 us (40%)
  starting transfers between devices  11.5 us (30%)
  Pallas kernels  8.73 us (23%)
  local copies, waits for them, and re-layouts  1.85 us (5%)
  between operations  0.79 us (2%)
    ppermute x6, waiting for transfers between devices, columns_path(): lax.ppermute(send, 'gx', pair)  10.5 us
    ppermute x6, starting transfers between devices, columns_path(): lax.ppermute(send, 'gx', pair)  8.9 us
    ppermute x1, waiting for transfers between devices, columns_path(): lax.ppermute(outer, ('gy', 'row'), cross + [(b, a) for a, b in cross])  4.74 us
    pallas_call x1, Pallas kernels, columns_path(): call(functools.partial(middle_kernel, plan), [out] * parts, [planes], flo...  4.39 us
    ppermute x1, starting transfers between devices, columns_path(): lax.ppermute(outer, ('gy', 'row'), cross + [(b, a) for a, b in cross])  2.53 us
    pallas_call x1, Pallas kernels, columns_path(): call(functools.partial(last_kernel, plan), [result, result], [pltpu.VMEM(...  2.14 us
    unnamed x13, local copies, waits for them, and re-layouts  1.85 us
    pallas_call x1, Pallas kernels, columns_path(): call(functools.partial(first_kernel, plan), [block, jax.ShapeDtypeStruct(...  1.32 us
  transfers between devices with their start and end apart: 8, of which 5 were waited for; matrix products, arithmetic and copies ran while one was open for 0% of the time, Pallas kernels for 1%

profile of v1, /device:TPU:2, one launch (start us, length us, event | category | flops | bytes accessed | tf_op | source)
XLA Modules:
  0.0 38.1 jit_solution(3539689370339730439)
XLA Ops:
  0.6 0.0 copy-start
  0.6 0.0 copy-start.2
  0.7 0.0 copy-start.1
  0.7 0.0 copy-start.4
  0.7 0.0 copy-start.5
  0.7 1.2 %copy.9.orders = s32[1024,64]{1,0:T(8,128)S(1)} copy(s32[1024,64]{0,1:T(8,128)} %param.12) | data formatting | bytes 524288 | tf_op args[5]
  1.9 0.0 copy-start.3
  1.9 0.0 copy-done
  1.9 0.0 copy-done.2
  1.9 0.0 copy-done.1
  1.9 0.6 %copy-done.3 = f32[1024]{0:T(1024)S(1)} copy-done((f32[1024]{0:T(1024)S(1)}, f32[1024]{0:T(1024)}, u32[]{:S(2)}) %copy-start.3) | copy-done | bytes 4120
  2.6 1.3 %shard_map.86 = (f32[144,128]{1,0:T(8,128)S(1)}, f32[8,256]{1,0:T(8,128)S(1)}, f32[144,128]{1,0:T(8,128)S(1)}, f32[144,128]{1,0:T(8,128)S(1)}, f32[144,128]{1,0:T(8,128)S(1)}) custom-call(f32[256,128]{1,0:T(8,128)S(1)} %bitcast.9, f32[256,128]{1,0:T(8,128)S(1)} %bitcast.11, f32[4,128]{1,0:T(4,128)S(1)} %copy-done.4, s32[4,128]{1,0:T(4,128)S(1)} %copy-done.5, ...), custom_call_target="tpu_custom_call" | custom-call | flops 268435456 | bytes 1048576 | tf_op jit(solution)/shard_map/pallas_call | solution.py:431
  3.9 1.6 %collective-permute-start = (f32[144,128]{1,0:T(8,128)S(1)}, f32[144,128]{1,0:T(8,128)S(1)}, u32[]{:S(2)}, u32[]{:S(2)}) collective-permute-start(f32[144,128]{1,0:T(8,128)S(1)} %get-tuple-element.20), channel_id=1, source_target_pairs={{0,4},{4,0},{8,12},{12,8},{1,5},{5,1},{9,13},{13,9},{2,6},{6,2},{1... | collective-permute-start | bytes 221192 | tf_op jit(solution)/shard_map/ppermute | solution.py:438
  5.5 2.6 %collective-permute-start.1 = (f32[144,128]{1,0:T(8,128)S(1)}, f32[144,128]{1,0:T(8,128)S(1)}, u32[]{:S(2)}, u32[]{:S(2)}) collective-permute-start(f32[144,128]{1,0:T(8,128)S(1)} %get-tuple-element.21), channel_id=1, source_target_pairs={{0,8},{4,12},{8,0},{12,4},{1,9},{5,13},{9,1},{13,5},{2,10},{6,14},... | collective-permute-start | bytes 221192 | tf_op jit(solution)/shard_map/ppermute | solution.py:438
  8.1 0.2 collective-permute-start.2
  8.4 0.0 collective-permute-done.refs_1_
  8.4 5.0 %collective-permute-done.1.refs_2_ = f32[144,128]{1,0:T(8,128)S(1)} collective-permute-done((f32[144,128]{1,0:T(8,128)S(1)}, f32[144,128]{1,0:T(8,128)S(1)}, u32[]{:S(2)}, u32[]{:S(2)}) %collective-permute-start.1) | collective-permute-done | bytes 73760 | tf_op jit(solution)/shard_map/ppermute | solution.py:438
  13.3 1.1 %collective-permute-done.2.refs_3_ = f32[144,128]{1,0:T(8,128)S(1)} collective-permute-done((f32[144,128]{1,0:T(8,128)S(1)}, f32[144,128]{1,0:T(8,128)S(1)}, u32[]{:S(2)}, u32[]{:S(2)}) %collective-permute-start.2) | collective-permute-done | bytes 73760 | tf_op jit(solution)/shard_map/ppermute | solution.py:438
  14.4 0.4 %shard_map.87 = (f32[520,128]{1,0:T(8,128)S(1)}, f32[520,128]{1,0:T(8,128)S(1)}) custom-call(f32[144,128]{1,0:T(8,128)S(1)} %get-tuple-element.19.refs_0_.own, f32[144,128]{1,0:T(8,128)S(1)} %collective-permute-done.refs_1_, f32[144,128]{1,0:T(8,128)S(1)} %collective-permute-done.1.refs_2_, f32[144,128]{1,0:T(8,128)S(1)} %collective-permute-done.2.refs_3_, ...), custom_call_target="tpu_custom_call" | custom-call | flops 67108864 | bytes 1048576 | tf_op jit(solution)/shard_map/pallas_call | solution.py:451
  14.8 0.1 collective-permute-start.3
  14.9 2.5 %collective-permute-start.4 = (f32[520,128]{1,0:T(8,128)S(1)}, f32[520,128]{1,0:T(8,128)S(1)}, u32[]{:S(2)}, u32[]{:S(2)}) collective-permute-start(f32[520,128]{1,0:T(8,128)S(1)} %get-tuple-element.25), channel_id=1, source_target_pairs={{1,2},{2,1},{5,6},{6,5},{9,10},{10,9},{13,14},{14,13},{17,18},{18,... | collective-permute-start | bytes 798728 | tf_op jit(solution)/shard_map/ppermute | solution.py:455
  17.5 0.4 %shard_map.88 = (bf16[1024,128]{1,0:T(8,128)(2,1)S(1)}, bf16[128,1024]{1,0:T(8,128)(2,1)S(1)}, bf16[1024,128]{1,0:T(8,128)(2,1)S(1)}, bf16[128,1024]{1,0:T(8,128)(2,1)S(1)}) custom-call(f32[1,1024]{1,0:T(1,128)S(1)} %bitcast.13, s32[1024,64]{1,0:T(8,128)S(1)} %copy.9.orders, s32[64,1024]{1,0:T(8,128)S(1)} %copy-done, ...), custom_call_target="tpu_custom_call" | custom-call | flops 67108864 | bytes 1048576 | tf_op jit(solution)/shard_map/pallas_call | solution.py:439
  17.9 0.0 collective-permute-done.3.refs_5_
  17.9 4.7 %collective-permute-done.4.refs_6_ = f32[520,128]{1,0:T(8,128)S(1)} collective-permute-done((f32[520,128]{1,0:T(8,128)S(1)}, f32[520,128]{1,0:T(8,128)S(1)}, u32[]{:S(2)}, u32[]{:S(2)}) %collective-permute-start.4) | collective-permute-done | bytes 266272 | tf_op jit(solution)/shard_map/ppermute | solution.py:455
  22.7 4.4 %shard_map.89 = (f32[128,128]{1,0:T(8,128)S(1)}, f32[128,128]{1,0:T(8,128)S(1)}, f32[128,128]{1,0:T(8,128)S(1)}, f32[128,128]{1,0:T(8,128)S(1)}) custom-call(f32[144,128]{1,0:T(8,128)S(1)} %get-tuple-element.19.refs_0_.own, f32[144,128]{1,0:T(8,128)S(1)} %collective-permute-done.refs_1_, f32[144,128]{1,0:T(8,128)S(1)} %collective-permute-done.1.refs_2_, ...), custom_call_target="tpu_custom_call" | custom-call | flops 536870912 | bytes 1048576 | tf_op jit(solution)/shard_map/pallas_call | solution.py:458
  27.1 1.1 %collective-permute-start.5 = (f32[128,128]{1,0:T(8,128)S(1)}, f32[128,128]{1,0:T(8,128)S(1)}, u32[]{:S(2)}, u32[]{:S(2)}) collective-permute-start(f32[128,128]{1,0:T(8,128)S(1)} %get-tuple-element.31), channel_id=1, source_target_pairs={{0,4},{4,0},{8,12},{12,8},{1,5},{5,1},{9,13},{13,9},{2,6},{6,2},{1... | collective-permute-start | bytes 196616 | tf_op jit(solution)/shard_map/ppermute | solution.py:461
  28.2 1.7 %collective-permute-start.6 = (f32[128,128]{1,0:T(8,128)S(1)}, f32[128,128]{1,0:T(8,128)S(1)}, u32[]{:S(2)}, u32[]{:S(2)}) collective-permute-start(f32[128,128]{1,0:T(8,128)S(1)} %get-tuple-element.32), channel_id=1, source_target_pairs={{0,8},{4,12},{8,0},{12,4},{1,9},{5,13},{9,1},{13,5},{2,10},{6,14},... | collective-permute-start | bytes 196616 | tf_op jit(solution)/shard_map/ppermute | solution.py:461
  29.9 1.6 %collective-permute-start.7 = (f32[128,128]{1,0:T(8,128)S(1)}, f32[128,128]{1,0:T(8,128)S(1)}, u32[]{:S(2)}, u32[]{:S(2)}) collective-permute-start(f32[128,128]{1,0:T(8,128)S(1)} %get-tuple-element.33), channel_id=1, source_target_pairs={{0,12},{4,8},{8,4},{12,0},{1,13},{5,9},{9,5},{13,1},{2,14},{6,10},... | collective-permute-start | bytes 196616 | tf_op jit(solution)/shard_map/ppermute | solution.py:461
  31.5 0.0 collective-permute-done.5.refs_1_
  31.5 2.6 %collective-permute-done.6.refs_2_ = f32[128,128]{1,0:T(8,128)S(1)} collective-permute-done((f32[128,128]{1,0:T(8,128)S(1)}, f32[128,128]{1,0:T(8,128)S(1)}, u32[]{:S(2)}, u32[]{:S(2)}) %collective-permute-start.6) | collective-permute-done | bytes 65568 | tf_op jit(solution)/shard_map/ppermute | solution.py:461
  34.1 1.9 %collective-permute-done.7.refs_3_ = f32[128,128]{1,0:T(8,128)S(1)} collective-permute-done((f32[128,128]{1,0:T(8,128)S(1)}, f32[128,128]{1,0:T(8,128)S(1)}, u32[]{:S(2)}, u32[]{:S(2)}) %collective-permute-start.7) | collective-permute-done | bytes 65568 | tf_op jit(solution)/shard_map/ppermute | solution.py:461
  36.0 2.1 %shard_map.90 = (f32[256,128]{1,0:T(8,128)}, f32[256,128]{1,0:T(8,128)}) custom-call(f32[128,128]{1,0:T(8,128)S(1)} %get-tuple-element.30.refs_0_, f32[128,128]{1,0:T(8,128)S(1)} %collective-permute-done.5.refs_1_, f32[128,128]{1,0:T(8,128)S(1)} %collective-permute-done.6.refs_2_, f32[128,128]{1,0:T(8,128)S(1)} %collective-permute-done.7.refs_3_, ...), custom_call_target="tpu_custom_call" | custom-call | flops 268435456 | bytes 1048576 | tf_op jit(solution)/shard_map/pallas_call | solution.py:463
  (2 shorter events, 0.0 us)
Async XLA Ops:
  0.6 1.3 %copy-start = (s32[64,1024]{1,0:T(8,128)S(1)}, s32[64,1024]{1,0:T(8,128)}, u32[]{:S(2)}) copy-start(s32[64,1024]{1,0:T(8,128)} %stoich.3) | copy-start | bytes 786436
  0.6 1.3 %copy-start.2 = (f32[64,1,4,128]{3,2,1,0:T(4,128)S(1)}, f32[64,1,4,128]{3,2,1,0:T(4,128)}, u32[]{:S(2)}) copy-start(f32[64,1,4,128]{3,2,1,0:T(4,128)} %param.8) | copy-start | bytes 393220
  0.7 1.3 %copy-start.1 = (f32[64,1,4,128]{3,2,1,0:T(4,128)S(1)}, f32[64,1,4,128]{3,2,1,0:T(4,128)}, u32[]{:S(2)}) copy-start(f32[64,1,4,128]{3,2,1,0:T(4,128)} %param.7) | copy-start | bytes 393220
  0.7 1.3 %copy-start.4 = (f32[4,128]{1,0:T(4,128)S(1)}, f32[4,128]{1,0:T(4,128)}, u32[]{:S(2)}) copy-start(f32[4,128]{1,0:T(4,128)} %cour.1) | copy-start | bytes 6148
  0.7 1.3 %copy-start.5 = (s32[4,128]{1,0:T(4,128)S(1)}, s32[4,128]{1,0:T(4,128)}, u32[]{:S(2)}) copy-start(s32[4,128]{1,0:T(4,128)} %direct.1) | copy-start | bytes 6148
  1.9 0.7 %copy-start.3 = (f32[1024]{0:T(1024)S(1)}, f32[1024]{0:T(1024)}, u32[]{:S(2)}) copy-start(f32[1024]{0:T(1024)} %param.11) | copy-start | bytes 12292
  3.9 4.5 %collective-permute-start = (f32[144,128]{1,0:T(8,128)S(1)}, f32[144,128]{1,0:T(8,128)S(1)}, u32[]{:S(2)}, u32[]{:S(2)}) collective-permute-start(f32[144,128]{1,0:T(8,128)S(1)} %get-tuple-element.20), channel_id=1, source_target_pairs={{0,4},{4,0},{8,12},{12,8},{1,5},{5,1},{9,13},{13,9},{2,6},{6,2},{1... | collective-permute-start | bytes 221192 | tf_op jit(solution)/shard_map/ppermute | solution.py:438
  5.5 7.8 %collective-permute-start.1 = (f32[144,128]{1,0:T(8,128)S(1)}, f32[144,128]{1,0:T(8,128)S(1)}, u32[]{:S(2)}, u32[]{:S(2)}) collective-permute-start(f32[144,128]{1,0:T(8,128)S(1)} %get-tuple-element.21), channel_id=1, source_target_pairs={{0,8},{4,12},{8,0},{12,4},{1,9},{5,13},{9,1},{13,5},{2,10},{6,14},... | collective-permute-start | bytes 221192 | tf_op jit(solution)/shard_map/ppermute | solution.py:438
  8.1 6.3 %collective-permute-start.2 = (f32[144,128]{1,0:T(8,128)S(1)}, f32[144,128]{1,0:T(8,128)S(1)}, u32[]{:S(2)}, u32[]{:S(2)}) collective-permute-start(f32[144,128]{1,0:T(8,128)S(1)} %get-tuple-element.22), channel_id=1, source_target_pairs={{0,12},{4,8},{8,4},{12,0},{1,13},{5,9},{9,5},{13,1},{2,14},{6,10},... | collective-permute-start | bytes 221192 | tf_op jit(solution)/shard_map/ppermute | solution.py:438
  14.8 3.1 %collective-permute-start.3 = (f32[520,128]{1,0:T(8,128)S(1)}, f32[520,128]{1,0:T(8,128)S(1)}, u32[]{:S(2)}, u32[]{:S(2)}) collective-permute-start(f32[520,128]{1,0:T(8,128)S(1)} %get-tuple-element.24), channel_id=1, source_target_pairs={{0,1},{1,0},{2,3},{3,2},{4,5},{5,4},{6,7},{7,6},{8,9},{9,8},{10,11... | collective-permute-start | bytes 798728 | tf_op jit(solution)/shard_map/ppermute | solution.py:456
  14.9 7.7 %collective-permute-start.4 = (f32[520,128]{1,0:T(8,128)S(1)}, f32[520,128]{1,0:T(8,128)S(1)}, u32[]{:S(2)}, u32[]{:S(2)}) collective-permute-start(f32[520,128]{1,0:T(8,128)S(1)} %get-tuple-element.25), channel_id=1, source_target_pairs={{1,2},{2,1},{5,6},{6,5},{9,10},{10,9},{13,14},{14,13},{17,18},{18,... | collective-permute-start | bytes 798728 | tf_op jit(solution)/shard_map/ppermute | solution.py:455
  27.1 4.5 %collective-permute-start.5 = (f32[128,128]{1,0:T(8,128)S(1)}, f32[128,128]{1,0:T(8,128)S(1)}, u32[]{:S(2)}, u32[]{:S(2)}) collective-permute-start(f32[128,128]{1,0:T(8,128)S(1)} %get-tuple-element.31), channel_id=1, source_target_pairs={{0,4},{4,0},{8,12},{12,8},{1,5},{5,1},{9,13},{13,9},{2,6},{6,2},{1... | collective-permute-start | bytes 196616 | tf_op jit(solution)/shard_map/ppermute | solution.py:461
  28.2 5.9 %collective-permute-start.6 = (f32[128,128]{1,0:T(8,128)S(1)}, f32[128,128]{1,0:T(8,128)S(1)}, u32[]{:S(2)}, u32[]{:S(2)}) collective-permute-start(f32[128,128]{1,0:T(8,128)S(1)} %get-tuple-element.32), channel_id=1, source_target_pairs={{0,8},{4,12},{8,0},{12,4},{1,9},{5,13},{9,1},{13,5},{2,10},{6,14},... | collective-permute-start | bytes 196616 | tf_op jit(solution)/shard_map/ppermute | solution.py:461
  29.9 6.1 %collective-permute-start.7 = (f32[128,128]{1,0:T(8,128)S(1)}, f32[128,128]{1,0:T(8,128)S(1)}, u32[]{:S(2)}, u32[]{:S(2)}) collective-permute-start(f32[128,128]{1,0:T(8,128)S(1)} %get-tuple-element.33), channel_id=1, source_target_pairs={{0,12},{4,8},{8,4},{12,0},{1,13},{5,9},{9,5},{13,1},{2,14},{6,10},... | collective-permute-start | bytes 196616 | tf_op jit(solution)/shard_map/ppermute | solution.py:461
